TPU v7x, 32 devices: a whole 2x2x4 slice. The times are simulated.
32 devices in a mesh: dp: 8 (over z, x), seq: 4 (over y, core).
Axes of the slice: x: 2, y: 2, z: 4, core: 2. Of those that a mesh axis runs over, the one named last changes fastest.
Arguments:
- tokens: bfloat16 [8, 1024, 1600], P('dp', 'seq'), may hold values from -6 to 6
- cotangent: bfloat16 [8, 1024, 1600], P('dp', 'seq'), may hold values from -6 to 6
- lengths: int32 [8], P('dp'), may hold values from 256 to 1024, as said below
- w_qkv: bfloat16 [7680000], P(('dp', 'seq')), may hold values from -0.15625 to 0.15625
- w_out: bfloat16 [2560000], P(('dp', 'seq')), may hold values from -2.5 to 2.5
- w_fc: bfloat16 [10246400], P(('dp', 'seq')), may hold values from -0.15625 to 0.15625
- w_proj: bfloat16 [10240000], P(('dp', 'seq')), may hold values from -0.078125 to 0.078125
- attention_vectors: bfloat16 [6400], P(('dp', 'seq')), as said below
- block_vectors: bfloat16 [6400], P(('dp', 'seq')), as said below
Outputs:
- output: bfloat16 [8, 1024, 1600], P('dp', 'seq')
- input_grad: float32 [8, 1024, 1600], P('dp', 'seq')
- grad_qkv: float32 [7680000], P(('dp', 'seq'))
- grad_out: float32 [2560000], P(('dp', 'seq'))
- grad_fc: float32 [10246400], P(('dp', 'seq'))
- grad_proj: float32 [10240000], P(('dp', 'seq'))
- grad_attention_vectors: float32 [6400], P(('dp', 'seq'))
- grad_block_vectors: float32 [6400], P(('dp', 'seq'))
Inputs may be any that keep to these rules, and one draw needn't show every extreme that they name: `lengths`: valid positions of each slot; in every draw one slot has all 1024 and one has 256. `attention_vectors`: gains near one, biases of order one half. `block_vectors`: gains near one, biases of order one half.
All inputs are finite; a program needn't handle non-finite values.
Results may differ from a plain program's by a relative error of at most 0.01.
Values may be sent and summed in bfloat16 or wider, within the bound.
No kernel may reach another device: no remote copies, remote signals or barrier semaphores. Data moves between devices by JAX's collectives and lax.ppermute only.
A program may use at most 448 MiB of HBM per device.

v0:
```python
from functools import partial
import jax
import jax.numpy as jnp
from jax import lax
from jax.sharding import PartitionSpec as P

HD = 64
EPS = 1e-05


def layer_norm(value, gain, shift):
    centre = value - jnp.mean(value, axis=-1, keepdims=True)
    spread = jnp.mean(centre * centre, axis=-1, keepdims=True)
    return centre * lax.rsqrt(spread + EPS) * gain + shift


def tanh_gelu(value):
    return jax.nn.gelu(value, approximate=True)


def split_weights(gathered, width):
    flat_qkv, flat_out, flat_fc, flat_proj, first_vectors, second_vectors = gathered
    hidden = flat_fc.shape[0] // (width + 1)
    expand_full = flat_fc.reshape(width + 1, hidden)
    token_rows = (
        jnp.concatenate([first_vectors, second_vectors]).astype(jnp.float32).reshape(8, width)
    )
    expand_bias = expand_full[width].astype(jnp.float32)
    return (
        flat_qkv.reshape(width, 3 * width),
        flat_out.reshape(width, width),
        expand_full[:width],
        flat_proj.reshape(hidden, width),
        token_rows,
        expand_bias,
    )


def to_heads(value, heads):
    slots, count, width = value.shape
    return jnp.moveaxis(value.reshape(slots, count, heads, width // heads), 2, 0)


def from_heads(value):
    heads, slots, count, size = value.shape
    return jnp.moveaxis(value, 0, 2).reshape(slots, count, heads * size)


def head_scores(allowed, query, keys):
    scores = jnp.einsum("sqd,skd->sqk", query, keys, preferred_element_type=jnp.float32) * 0.125
    return jnp.where(allowed, scores, -1e30)


def head_forward(allowed, item):
    query, keys, values = item
    scores = head_scores(allowed, query, keys)
    peak = jnp.max(scores, axis=-1, keepdims=True)
    raised = jnp.exp(scores - peak)
    total = jnp.sum(raised, axis=-1, keepdims=True)
    weights = (raised / total).astype(jnp.bfloat16)
    result = jnp.einsum("sqk,skd->sqd", weights, values, preferred_element_type=jnp.float32)
    return (result, (peak + jnp.log(total))[..., 0])


def head_backward(allowed, item):
    query, keys, values, grad_result, normal = item
    scores = head_scores(allowed, query, keys)
    probs = jnp.where(allowed, jnp.exp(scores - normal[..., None]), 0.0)
    weights = probs.astype(jnp.bfloat16)
    grad_probs = jnp.einsum("sqd,skd->sqk", grad_result, values, preferred_element_type=jnp.float32)
    inner_total = jnp.sum(probs * grad_probs, axis=-1, keepdims=True)
    grad_scores = (probs * (grad_probs - inner_total) * 0.125).astype(jnp.bfloat16)
    grad_query = jnp.einsum("sqk,skd->sqd", grad_scores, keys, preferred_element_type=jnp.float32)
    grad_keys = jnp.einsum("sqk,sqd->skd", grad_scores, query, preferred_element_type=jnp.float32)
    grad_values = jnp.einsum(
        "sqk,sqd->skd", weights, grad_result, preferred_element_type=jnp.float32
    )
    return (grad_query, grad_keys, grad_values)


def local(tokens, cotangent, lengths, w_qkv, w_out, w_fc, w_proj, attention_vectors, block_vectors):
    slots, count, width = tokens.shape
    heads = width // HD
    rank = lax.axis_index("seq")
    span = count * lax.axis_size("seq")
    part_qkv, part_out, part_fc, part_proj, part_first, part_second = (
        lax.all_gather(w_qkv, "seq", axis=0, tiled=True),
        lax.all_gather(w_out, "seq", axis=0, tiled=True),
        lax.all_gather(w_fc, "seq", axis=0, tiled=True),
        lax.all_gather(w_proj, "seq", axis=0, tiled=True),
        lax.all_gather(attention_vectors, "seq", axis=0, tiled=True),
        lax.all_gather(block_vectors, "seq", axis=0, tiled=True),
    )
    gathered = (
        lax.all_gather(part_qkv, "dp", axis=0, tiled=True),
        lax.all_gather(part_out, "dp", axis=0, tiled=True),
        lax.all_gather(part_fc, "dp", axis=0, tiled=True),
        lax.all_gather(part_proj, "dp", axis=0, tiled=True),
        lax.all_gather(part_first, "dp", axis=0, tiled=True),
        lax.all_gather(part_second, "dp", axis=0, tiled=True),
    )
    (
        query_key_value_weight,
        output_weight,
        expand_weight,
        contract_weight,
        token_rows,
        expand_bias,
    ) = split_weights(gathered, width)
    place = rank * count + jnp.arange(count)
    key_place = jnp.arange(span)
    allowed = (key_place[None, None, :] <= place[None, :, None]) & (
        key_place[None, None, :] < lengths[:, None, None]
    )
    valid = place[None, :] < lengths[:, None]
    source = tokens.astype(jnp.float32)
    normed_low = layer_norm(source, token_rows[0], token_rows[1]).astype(jnp.bfloat16)
    mixed_heads = jnp.einsum(
        "scd,de->sce", normed_low, query_key_value_weight, preferred_element_type=jnp.float32
    )
    query = (mixed_heads[..., :width] + token_rows[2]).astype(jnp.bfloat16)
    keys = mixed_heads[..., width : 2 * width].astype(jnp.bfloat16)
    values = (mixed_heads[..., 2 * width :] + token_rows[3]).astype(jnp.bfloat16)
    all_keys, all_values = (
        lax.all_gather(keys, "seq", axis=1, tiled=True),
        lax.all_gather(values, "seq", axis=1, tiled=True),
    )
    query_heads = to_heads(query, heads)
    key_heads = to_heads(all_keys, heads)
    value_heads = to_heads(all_values, heads)
    head_result, normal = lax.map(
        partial(head_forward, allowed), (query_heads, key_heads, value_heads)
    )
    attention_output = from_heads(head_result).astype(jnp.bfloat16)
    middle_state = (
        source
        + jnp.einsum(
            "scd,de->sce", attention_output, output_weight, preferred_element_type=jnp.float32
        )
        + token_rows[4]
    )
    second_normed = layer_norm(middle_state, token_rows[5], token_rows[6]).astype(jnp.bfloat16)
    inner_hidden = (
        jnp.einsum("scd,df->scf", second_normed, expand_weight, preferred_element_type=jnp.float32)
        + expand_bias
    )
    active_low = tanh_gelu(inner_hidden).astype(jnp.bfloat16)
    result = (
        middle_state
        + jnp.einsum("scf,fd->scd", active_low, contract_weight, preferred_element_type=jnp.float32)
        + token_rows[7]
    )
    output = result.astype(jnp.bfloat16)
    again_qkv, again_out, again_fc, again_proj, again_first, again_second = (
        lax.all_gather(w_qkv, "seq", axis=0, tiled=True),
        lax.all_gather(w_out, "seq", axis=0, tiled=True),
        lax.all_gather(w_fc, "seq", axis=0, tiled=True),
        lax.all_gather(w_proj, "seq", axis=0, tiled=True),
        lax.all_gather(attention_vectors, "seq", axis=0, tiled=True),
        lax.all_gather(block_vectors, "seq", axis=0, tiled=True),
    )
    again = (
        lax.all_gather(again_qkv, "dp", axis=0, tiled=True),
        lax.all_gather(again_out, "dp", axis=0, tiled=True),
        lax.all_gather(again_fc, "dp", axis=0, tiled=True),
        lax.all_gather(again_proj, "dp", axis=0, tiled=True),
        lax.all_gather(again_first, "dp", axis=0, tiled=True),
        lax.all_gather(again_second, "dp", axis=0, tiled=True),
    )
    (
        query_key_value_weight,
        output_weight,
        expand_weight,
        contract_weight,
        token_rows,
        expand_bias,
    ) = split_weights(again, width)
    grad_result = cotangent * valid.astype(jnp.bfloat16)[..., None]
    grad_wide = grad_result.astype(jnp.float32)
    grad_proj = jnp.einsum(
        "scf,scd->fd", active_low, grad_result, preferred_element_type=jnp.float32
    )
    bias_proj_grad = jnp.sum(grad_wide, axis=(0, 1))
    grad_active = jnp.einsum(
        "scd,fd->scf", grad_result, contract_weight, preferred_element_type=jnp.float32
    )
    gelu_back = jax.vjp(tanh_gelu, inner_hidden)[1]
    inner_low = gelu_back(grad_active)[0].astype(jnp.bfloat16)
    bias_fc_grad = jnp.sum(inner_low.astype(jnp.float32), axis=(0, 1))
    grad_fc = jnp.einsum(
        "scd,scf->df", second_normed, inner_low, preferred_element_type=jnp.float32
    )
    grad_fc_full = jnp.concatenate([grad_fc, bias_fc_grad[None, :]], axis=0).reshape(-1)
    grad_normed_two = jnp.einsum(
        "scf,df->scd", inner_low, expand_weight, preferred_element_type=jnp.float32
    )
    norm_two_back = jax.vjp(layer_norm, middle_state, token_rows[5], token_rows[6])[1]
    grad_mid, gain_two_grad, shift_two_grad = norm_two_back(grad_normed_two)
    grad_mid = grad_mid + grad_wide
    branch_low = grad_mid.astype(jnp.bfloat16)
    bias_out_grad = jnp.sum(branch_low.astype(jnp.float32), axis=(0, 1))
    grad_out_mat = jnp.einsum(
        "scd,sce->de", attention_output, branch_low, preferred_element_type=jnp.float32
    )
    grad_attended = jnp.einsum(
        "sce,de->scd", branch_low, output_weight, preferred_element_type=jnp.float32
    ).astype(jnp.bfloat16)
    grad_query, grad_keys, grad_values = lax.map(
        partial(head_backward, allowed),
        (query_heads, key_heads, value_heads, to_heads(grad_attended, heads), normal),
    )
    keys_sum, values_sum = (
        lax.psum_scatter(from_heads(grad_keys), "seq", scatter_dimension=1, tiled=True),
        lax.psum_scatter(from_heads(grad_values), "seq", scatter_dimension=1, tiled=True),
    )
    query_low = from_heads(grad_query).astype(jnp.bfloat16)
    keys_low = keys_sum.astype(jnp.bfloat16)
    values_low = values_sum.astype(jnp.bfloat16)
    bias_query_grad = jnp.sum(query_low.astype(jnp.float32), axis=(0, 1))
    bias_value_grad = jnp.sum(values_low.astype(jnp.float32), axis=(0, 1))
    grad_mixed = jnp.concatenate([query_low, keys_low, values_low], axis=-1)
    grad_qkv = jnp.einsum("scd,sce->de", normed_low, grad_mixed, preferred_element_type=jnp.float32)
    grad_normed = jnp.einsum(
        "sce,de->scd", grad_mixed, query_key_value_weight, preferred_element_type=jnp.float32
    )
    norm_one_back = jax.vjp(layer_norm, source, token_rows[0], token_rows[1])[1]
    grad_source, gain_one_grad, shift_one_grad = norm_one_back(grad_normed)
    input_grad = grad_mid + grad_source
    first_grad = jnp.concatenate([gain_one_grad, shift_one_grad, bias_query_grad, bias_value_grad])
    second_grad = jnp.concatenate([bias_out_grad, gain_two_grad, shift_two_grad, bias_proj_grad])
    qkv_part, out_part, fc_part, proj_part, first_part, second_part = (
        lax.psum_scatter(grad_qkv.reshape(-1), "dp", scatter_dimension=0, tiled=True),
        lax.psum_scatter(grad_out_mat.reshape(-1), "dp", scatter_dimension=0, tiled=True),
        lax.psum_scatter(grad_fc_full, "dp", scatter_dimension=0, tiled=True),
        lax.psum_scatter(grad_proj.reshape(-1), "dp", scatter_dimension=0, tiled=True),
        lax.psum_scatter(first_grad, "dp", scatter_dimension=0, tiled=True),
        lax.psum_scatter(second_grad, "dp", scatter_dimension=0, tiled=True),
    )
    qkv_shard, out_shard, fc_shard, proj_shard, first_shard, second_shard = (
        lax.psum_scatter(qkv_part, "seq", scatter_dimension=0, tiled=True),
        lax.psum_scatter(out_part, "seq", scatter_dimension=0, tiled=True),
        lax.psum_scatter(fc_part, "seq", scatter_dimension=0, tiled=True),
        lax.psum_scatter(proj_part, "seq", scatter_dimension=0, tiled=True),
        lax.psum_scatter(first_part, "seq", scatter_dimension=0, tiled=True),
        lax.psum_scatter(second_part, "seq", scatter_dimension=0, tiled=True),
    )
    return (
        output,
        input_grad,
        qkv_shard,
        out_shard,
        fc_shard,
        proj_shard,
        first_shard,
        second_shard,
    )


def solution(mesh):
    in_specs = (
        P("dp", "seq", None),
        P("dp", "seq", None),
        P("dp"),
        P(("dp", "seq")),
        P(("dp", "seq")),
        P(("dp", "seq")),
        P(("dp", "seq")),
        P(("dp", "seq")),
        P(("dp", "seq")),
    )
    out_specs = (
        P("dp", "seq", None),
        P("dp", "seq", None),
        P(("dp", "seq")),
        P(("dp", "seq")),
        P(("dp", "seq")),
        P(("dp", "seq")),
        P(("dp", "seq")),
        P(("dp", "seq")),
    )
    return jax.shard_map(local, mesh=mesh, in_specs=in_specs, out_specs=out_specs, check_vma=False)
```

profile of v0, /device:TPU:0, one launch (start us, length us, event | category | flops | bytes accessed | tf_op | source)
XLA Modules:
  0.0 6387.4 jit_solution(10073918586808207974)
XLA Ops:
  7.2 6.3 reshape.576
  15.8 5.9 dynamic-update-slice.4
  23.4 25.4 all-gather.19.cloned.1.call-done
  49.0 8.1 reshape.584
  57.3 19.0 all-gather.2
  77.1 40.4 all-reduce.29.cloned.1.call-done
  117.4 7.4 broadcast.247
  124.8 39.2 dynamic-update-slice.5
  166.0 6.0 all-reduce.23
  172.5 51.9 all-reduce.22
  226.2 478.7 %all-gather.21.cloned.1.call-done = bf16[8,1,960000]{2,1,0:T(2,128)(2,1)} async-done(((bf16[1,1,960000]{2,1,0:T(2,128)(2,1)}), bf16[8,1,960000]{2,1,0:T(2,128)(2,1)}) %all-gather.21.cloned.1.call-update) | async-done | bytes 15360016 | tf_op jit(solution)/shard_map/all_gather | solution.py:95
  704.9 325.4 %reduce.24 = bf16[8,960000]{1,0:T(8,128)(2,1)} reduce(bf16[8,1,960000]{2,1,0:T(2,128)(2,1)} %all-gather.21.cloned.1.call-done, bf16[]{:T(256)} %constant.172), dimensions={1}, to_apply=%all-gather.1.reduce_sub_computation | reduce | bytes 30720002 | tf_op jit(solution)/shard_map/all_gather | solution.py:95
  1030.3 34.2 reshape.626
  1064.5 25.2 reshape.541
  1089.7 14.8 convolution_bitcast_fusion.4
  1110.4 17.7 reduce.26
  1133.1 32.0 reduce.25
  1165.2 12.3 reshape.628
  1177.5 9.6 reshape.545
  1187.1 325.9 %all-reduce.31.cloned.1.call-done = bf16[10246400]{0:T(1024)(128)(2,1)} async-done(((bf16[10246400]{0:T(1024)(128)(2,1)}), bf16[10246400]{0:T(1024)(128)(2,1)}) %all-reduce.31.cloned.1.call-update) | async-done | bytes 20492816
  1513.1 16.9 slice.87
  1530.0 35.4 slice.74
  1568.0 7.0 copy.27
  1576.0 7.1 copy.28
  1583.3 79.7 %while.28 = (s32[]{:T(128)}, bf16[25,1,256,64]{2,3,1,0:T(8,128)(2,1)S(1)}, f32[25,1,256]{2,1,0:T(1,128)S(1)}, bf16[25,1,256,64]{3,2,1,0:T(8,128)(2,1)}, bf16[25,...) while((s32[]{:T(128)}, ...), condition=%wide.region_5.6_spmd.clone, body=%wide.region_2.5_spmd.clone.sunk | while | flops 69730048 | bytes 3815529 | solution.py:131
  1663.0 5.3 fusion.110
  1668.6 12.4 convolution_add_fusion
  1681.0 289.2 %all-gather.17.cloned.1.call-done = bf16[10240000]{0:T(1024)(128)(2,1)} async-done(((bf16[1280000]{0:T(1024)(128)(2,1)}), bf16[10240000]{0:T(1024)(128)(2,1)}) %all-gather.17.cloned.1.call-update) | async-done | bytes 20480016 | tf_op jit(solution)/shard_map/all_gather | solution.py:98
  1970.3 34.0 reshape.547
  2004.2 14.1 convert_reduce_fusion
  2018.3 13.4 fusion.74
  2039.8 200.8 %while.29 = (s32[]{:T(128)}, bf16[25,1,256,64]{2,3,1,0:T(8,128)(2,1)S(1)}, f32[25,1,1024,64]{2,3,1,0:T(8,128)}, f32[25,1,1024,64]{2,3,1,0:T(8,128)}, bf16[25,1,2...) while((s32[]{:T(128)}, ...), condition=%wide.region_12.13_spmd.clone, body=%wide.region_10.12_spmd.clone.sunk | while | flops 171179776 | bytes 9515137 | solution.py:208
  2241.4 22.7 fusion.84
  2264.1 48.3 reshape.557
  2312.4 7.0 fusion.81
  2319.4 13.5 reshape.555
  2332.8 18.4 fusion.101
  2351.2 28.1 pad_maximum_fusion
  2379.3 39.9 reshape.556
  2424.4 13.8 fusion.77
  2438.2 36.5 reshape.554
  2477.1 3609.6 %all-reduce.33.cloned.1.call-done = (f32[7680000]{0:T(1024)}, f32[2560000]{0:T(1024)}, f32[10246400]{0:T(1024)}, f32[10240000]{0:T(1024)}) async-done(((f32[7680000]{0:T(1024)}, f32[2560000]{0:T(1024)}, f32[10246400]{0:T(1024)}, f32[10240000]{0:T(1024)}), (f32[7680000]{0:T(1024)}, f32[2560000]{0:T(1024)}, f32[10246400]{0:T(1024)}, f32[10240000]{0:T(1024)})) %all-reduce.33.cloned.1.call-update) | async-done | bytes 122905616
  6086.8 5.1 dynamic-slice.7
  6110.5 17.3 fusion.60
  6127.8 8.2 fusion.71
  6137.3 35.6 all-reduce.18
  6173.1 6.4 all-reduce.20
  6184.1 186.5 %all-reduce.35.cloned.1.call-done = (f32[960000]{0:T(1024)}, f32[320000]{0:T(1024)}, f32[1280800]{0:T(1024)}, f32[1280000]{0:T(1024)}) async-done(((f32[960000]{0:T(1024)}, f32[320000]{0:T(1024)}, f32[1280800]{0:T(1024)}, f32[1280000]{0:T(1024)}), (f32[960000]{0:T(1024)}, f32[320000]{0:T(1024)}, f32[1280800]{0:T(1024)}, f32[1280000]{0:T(1024)})) %all-reduce.35.cloned.1.call-update) | async-done | bytes 15363216
  (465 shorter events, 344.2 us)
Async XLA Ops:
  7.2 8.7 copy-start.12
  7.2 41.7 all-gather.19.cloned.1.call-start
  13.5 103.9 %all-reduce.29.cloned.1.call-start = ((), (), s32[]{:S(2)}) async-start(), calls=%async_computation.7 | async-start | bytes 5124096
  21.7 1.6 copy-start.3
  21.7 27.2 copy-start.13
  23.4 681.5 %all-gather.21.cloned.1.call-start = ((), (), s32[]{:S(2)}) async-start(), calls=%async_computation.10 | async-start | bytes 34560000 | tf_op jit(solution)/shard_map/all_gather | solution.py:95
  48.9 8.2 copy-start.16
  48.9 1061.5 %all-gather.25.cloned.1.call-start = ((), (), s32[]{:S(2)}) async-start(), calls=%async_computation.12 | async-start | bytes 6400000 | tf_op jit(solution)/shard_map/all_gather | solution.py:90
  57.1 1076.1 %all-gather.23.cloned.1.call-start = ((), (), s32[]{:S(2)}) async-start(), calls=%async_computation.11 | async-start | bytes 11520000 | tf_op jit(solution)/shard_map/all_gather | solution.py:96
  76.4 1436.7 %all-reduce.31.cloned.1.call-start = ((), (), s32[]{:S(2)}) async-start(), calls=%async_computation.8 | async-start | bytes 40988672
  117.4 7.4 copy-start.11
  164.0 1.5 copy-start.33
  164.0 1.7 copy-start.34
  164.0 60.4 copy-start
  164.0 1403.9 %all-gather.13.cloned.1.call-start = ((), (), s32[]{:S(2)}) async-start(), calls=%async_computation.2 | async-start | bytes 4096000 | tf_op jit(solution)/shard_map/all_gather | solution.py:125
  224.6 865.1 %copy-start.19 = (f32[256]{0:T(256)}, f32[256]{0:T(256)S(1)}, u32[]{:S(2)}) copy-start(f32[256]{0:T(256)S(1)} %broadcast_multiply_fusion.1) | copy-start | bytes 3076
  224.9 0.6 copy-start.27
  224.9 864.8 %copy-start.21 = (f32[256]{0:T(256)}, f32[256]{0:T(256)S(1)}, u32[]{:S(2)}) copy-start(f32[256]{0:T(256)S(1)} %fusion.95) | copy-start | bytes 3076
  226.2 863.5 %copy-start.14 = (f32[1600]{0:T(1024)}, f32[1600]{0:T(1024)S(1)}, u32[]{:S(2)}) copy-start(f32[1600]{0:T(1024)S(1)} %get-tuple-element.229) | copy-start | bytes 19204
  226.2 863.6 %copy-start.17 = (f32[1600]{0:T(1024)}, f32[1600]{0:T(1024)S(1)}, u32[]{:S(2)}) copy-start(f32[1600]{0:T(1024)S(1)} %get-tuple-element.228) | copy-start | bytes 19204
  1107.0 469.1 %all-gather.15.cloned.1.call-start = ((), (), s32[]{:S(2)}) async-start(), calls=%async_computation.3 | async-start | bytes 4096000 | tf_op jit(solution)/shard_map/all_gather | solution.py:126
  1110.4 859.9 %all-gather.17.cloned.1.call-start = ((), (), s32[]{:S(2)}) async-start(), calls=%async_computation.4 | async-start | bytes 23040000 | tf_op jit(solution)/shard_map/all_gather | solution.py:98
  1132.3 1286.9 %reduce-scatter.3.cloned.1.call-start = ((), (), s32[]{:S(2)}) async-start(), calls=%async_computation.5 | async-start | bytes 8192000 | tf_op jit(solution)/shard_map/reduce_scatter | solution.py:213
  1133.1 1108.3 %copy-start.31 = (bf16[256]{0:T(256)(128)(2,1)}, bf16[256]{0:T(256)(128)(2,1)S(1)}, u32[]{:S(2)}) copy-start(bf16[256]{0:T(256)(128)(2,1)S(1)} %compare_convert_fusion) | copy-start | bytes 1540
  1663.0 5.3 copy-start.7
  1681.0 323.2 %copy-start.4 = (bf16[1,256,1600]{1,2,0:T(8,128)(2,1)S(1)}, bf16[1,256,1600]{1,2,0:T(8,128)(2,1)}, u32[]{:S(2)}) copy-start(bf16[1,256,1600]{1,2,0:T(8,128)(2,1)} %param.14) | copy-start | bytes 2457604
  2031.7 1.7 copy-start.6
  2032.2 5.7 copy-start.2
  2032.2 5.7 copy-start.25
  2033.5 4.5 copy-start.10
  2240.6 181.1 %reduce-scatter.5.cloned.1.call-start = ((), (), s32[]{:S(2)}) async-start(), calls=%async_computation.6 | async-start | bytes 8192000 | tf_op jit(solution)/shard_map/reduce_scatter | solution.py:214
  2241.3 3845.4 %all-reduce.33.cloned.1.call-start = ((), (), s32[]{:S(2)}) async-start(), calls=%async_computation.13 | async-start | bytes 245817344
  2264.1 48.3 copy-start.8
  2419.2 5.2 copy-start.1
  2419.2 5.2 copy-start.15
  2419.2 5.2 copy-start.18
  2419.2 5.2 copy-start.20
  2419.2 5.2 copy-start.22
  2423.5 0.9 copy-start.9
  2474.8 3895.8 %all-reduce.35.cloned.1.call-start = ((), (), s32[]{:S(2)}) async-start(), calls=%async_computation.14 | async-start | bytes 30736384
  6103.8 6.6 copy-start.23
  6103.8 6.6 copy-start.24
  6103.8 6.6 copy-start.30
  6103.8 6.7 copy-start.29
  6127.8 8.6 copy-start.28
  6136.0 44.8 copy-start.5
  6136.0 44.8 copy-start.26
  6136.1 44.7 copy-start.32
Sparse Core Ops, SparseCore 0:
  13.6 35.2 all-gather.18
  51.3 66.0 all-reduce.28
  119.0 585.7 all-gather.20
  706.9 39.7 all-gather.24
  749.0 147.8 all-gather.22
  901.4 611.6 all-reduce.30
  1515.3 28.8 all-gather.12
  1546.3 29.6 all-gather.14
  1577.7 392.5 all-gather.16
  2240.7 60.0 reduce-scatter.2
  2303.4 60.0 reduce-scatter.4
  2474.9 3611.7 all-reduce.32
  6103.9 266.6 all-reduce.34
where the time goes:
time: 6410 us; the launch traced here: 6390 us
  waiting for transfers between devices  4960 us (77%)
  other arithmetic  434 us (7%)
  local copies, waits for them, and re-layouts  433 us (7%)
  matrix products  418 us (7%)
  blocking collectives  119 us (2%)
    unnamed x17, waiting for transfers between devices  4160 us
    all_gather x1, waiting for transfers between devices, local(): lax.all_gather(part_qkv, 'dp', axis=0, tiled=True)  479 us
    all_gather x1, other arithmetic, local(): lax.all_gather(part_qkv, 'dp', axis=0, tiled=True)  325 us
    all_gather x1, waiting for transfers between devices, local(): lax.all_gather(part_proj, 'dp', axis=0, tiled=True)  289 us
    unnamed x101, local copies, waits for them, and re-layouts  152 us
  transfers between devices with their start and end apart: 13, of which 8 were waited for; matrix products, arithmetic and copies ran while one was open for 15% of the time, Pallas kernels for 0%

commit v1 on v0

--- a/solution.py
+++ b/solution.py
@@ -1,3 +1,4 @@
+import functools
 from functools import partial
 import jax
 import jax.numpy as jnp
@@ -6,6 +7,22 @@
 
 HD = 64
 EPS = 1e-05
+
+
+def replace_stops_all(incoming_x, link_axis):
+    shares = lax.axis_size(link_axis)
+    line_up = tuple(((jj, (jj + 1) % shares) for jj in range(shares)))
+    fields = tuple(((jj, (jj - 1) % shares) for jj in range(shares)))
+    o_now, current_block = ([incoming_x], [incoming_x])
+    for _ in range(shares // 2):
+        o_now.append(lax.ppermute(o_now[-1], link_axis, line_up))
+    for _ in range((shares - 1) // 2):
+        current_block.append(lax.ppermute(current_block[-1], link_axis, fields))
+    v_now = jnp.concatenate([*o_now[::-1], *current_block[1:]], 0)
+    return jnp.roll(v_now, (lax.axis_index(link_axis) - shares // 2) * incoming_x.shape[0], 0)
+
+
+try_all_lots_all_on = functools.partial(replace_stops_all, link_axis="dp")
 
 
 def layer_norm(value, gain, shift):
@@ -92,7 +109,7 @@
         lax.all_gather(block_vectors, "seq", axis=0, tiled=True),
     )
     gathered = (
-        lax.all_gather(part_qkv, "dp", axis=0, tiled=True),
+        try_all_lots_all_on(part_qkv),
         lax.all_gather(part_out, "dp", axis=0, tiled=True),
         lax.all_gather(part_fc, "dp", axis=0, tiled=True),
         lax.all_gather(part_proj, "dp", axis=0, tiled=True),

time: 6410 us -> 7350 us (1.15)
  local copies, waits for them, and re-layouts: 433 us -> 957 us
  waiting for transfers between devices: 4960 us -> 5210 us
    unnamed x101 -> x125, local copies, waits for them, and re-layouts: 152 us -> 608 us
    ppermute x0 -> x7, waiting for transfers between devices: none -> 259 us  [the longest x4 252 us: replace_stops_all(): o_now.append(lax.ppermute(o_now[-1], link_axis, line_up))]
    unnamed x17, waiting for transfers between devices: 4160 us -> 4060 us
    all_gather x1, waiting for transfers between devices: 479 us -> 564 us  [local(): lax.all_gather(again_qkv, 'dp', axis=0, tiled=True)]
    all_gather x1 -> x2, other arithmetic: 325 us -> 362 us  [the longest x1 325 us: local(): lax.all_gather(again_qkv, 'dp', axis=0, tiled=True)]
  transfers between devices with their start and end apart: 13 -> 20, of which waited for: 8 -> 9; matrix products, arithmetic and copies ran while one was open for 15% -> 21% of each run, Pallas kernels for 0% -> 0%
where the time goes in v1:
time: 7350 us; the launch traced here: 7280 us
  waiting for transfers between devices  5210 us (71%)
  local copies, waits for them, and re-layouts  957 us (13%)
  other arithmetic  469 us (6%)
  matrix products  417 us (6%)
  blocking collectives  155 us (2%)
    unnamed x17, waiting for transfers between devices  4060 us
    unnamed x125, local copies, waits for them, and re-layouts  608 us
    all_gather x1, waiting for transfers between devices, local(): lax.all_gather(again_qkv, 'dp', axis=0, tiled=True)  564 us
    all_gather x1, waiting for transfers between devices, local(): lax.all_gather(part_proj, 'dp', axis=0, tiled=True)  328 us
    all_gather x1, other arithmetic, local(): lax.all_gather(again_qkv, 'dp', axis=0, tiled=True)  325 us
    ppermute x4, waiting for transfers between devices, replace_stops_all(): o_now.append(lax.ppermute(o_now[-1], link_axis, line_up))  252 us
  transfers between devices with their start and end apart: 20, of which 9 were waited for; matrix products, arithmetic and copies ran while one was open for 21% of the time, Pallas kernels for 0%

profile of v1, /device:TPU:0, one launch (start us, length us, event | category | flops | bytes accessed | tf_op | source)
XLA Modules:
  0.0 7280.3 jit_solution(2126792709130679528)
XLA Ops:
  31.3 20.2 all-gather.1
  55.7 37.1 reduce.24
  98.6 45.4 collective-permute-done
  150.1 91.1 %collective-permute-done.1 = bf16[960000]{0:T(1024)(128)(2,1)S(1)} collective-permute-done((bf16[960000]{0:T(1024)(128)(2,1)S(1)}, bf16[960000]{0:T(1024)(128)(2,1)S(1)}, u32[]{:S(2)}, u32[]{:S(2)}) %collective-permute-start.1) | collective-permute-done | bytes 1920032 | tf_op jit(solution)/shard_map/ppermute | solution.py:18
  251.2 115.6 %collective-permute-done.2 = bf16[960000]{0:T(1024)(128)(2,1)} collective-permute-done((bf16[960000]{0:T(1024)(128)(2,1)S(1)}, bf16[960000]{0:T(1024)(128)(2,1)}, u32[]{:S(2)}, u32[]{:S(2)}) %collective-permute-start.2) | collective-permute-done | bytes 1920032 | tf_op jit(solution)/shard_map/ppermute | solution.py:18
  376.4 24.5 collective-permute-start.6
  410.6 84.8 %all-reduce.22 = (bf16[6400]{0:T(1024)(128)(2,1)S(1)}, bf16[6400]{0:T(1024)(128)(2,1)S(1)}) all-reduce(bf16[6400]{0:T(1024)(128)(2,1)S(1)} %dynamic-update-slice.3, bf16[6400]{0:T(1024)(128)(2,1)S(1)} %dynamic-update-slice.1), channel_id=1, replica_groups=mesh['dp'=8,'seq'=4] {'dp'}, use_global_device_ids=true, to_apply=%add.3 | all-reduce | flops 12800 | bytes 51200
  497.2 30.0 dynamic-update-slice.6
  527.2 29.9 dynamic-update-slice.7
  557.1 30.0 dynamic-update-slice.8
  587.1 30.0 dynamic-update-slice.9
  617.1 29.9 dynamic-update-slice.10
  647.1 30.0 dynamic-update-slice.11
  677.1 29.9 dynamic-update-slice.12
  707.0 30.0 dynamic-update-slice.13
  737.1 30.0 dynamic-update-slice.14
  767.1 29.9 dynamic-update-slice.15
  797.0 30.0 dynamic-update-slice.16
  827.1 29.8 dynamic-update-slice.17
  856.9 30.0 dynamic-update-slice.18
  886.9 30.0 dynamic-update-slice.19
  916.9 29.9 dynamic-update-slice.20
  946.8 30.0 dynamic-update-slice.21
  989.8 25.1 reshape.543
  1014.9 14.7 convolution_bitcast_fusion.4
  1043.7 39.9 dynamic-update-slice.5
  1084.0 17.6 reduce.26
  1107.4 31.8 reduce.25
  1177.2 80.1 %while.28 = (s32[]{:T(128)}, bf16[25,1,256,64]{2,3,1,0:T(8,128)(2,1)S(1)}, f32[25,1,256]{2,1,0:T(1,128)S(1)}, bf16[25,1,256,64]{3,2,1,0:T(8,128)(2,1)}, bf16[25,...) while((s32[]{:T(128)}, ...), condition=%wide.region_5.6_spmd.clone, body=%wide.region_2.5_spmd.clone.sunk | while | flops 69730048 | bytes 3815529 | solution.py:148
  1262.8 447.9 %all-reduce.31.cloned.1.call-done = bf16[10246400]{0:T(1024)(128)(2,1)} async-done(((bf16[10246400]{0:T(1024)(128)(2,1)}), bf16[10246400]{0:T(1024)(128)(2,1)}) %all-reduce.31.cloned.1.call-update) | async-done | bytes 20492816
  1710.7 17.1 slice.87
  1727.8 35.3 slice.74
  1776.3 327.7 %all-gather.17.cloned.1.call-done = bf16[10240000]{0:T(1024)(128)(2,1)} async-done(((bf16[1280000]{0:T(1024)(128)(2,1)}), bf16[10240000]{0:T(1024)(128)(2,1)}) %all-gather.17.cloned.1.call-update) | async-done | bytes 20480016 | tf_op jit(solution)/shard_map/all_gather | solution.py:115
  2104.0 33.9 reshape.549
  2173.5 200.8 %while.29 = (s32[]{:T(128)}, bf16[25,1,256,64]{2,3,1,0:T(8,128)(2,1)S(1)}, f32[25,1,1024,64]{2,3,1,0:T(8,128)}, f32[25,1,1024,64]{2,3,1,0:T(8,128)}, bf16[25,1,2...) while((s32[]{:T(128)}, ...), condition=%wide.region_12.13_spmd.clone, body=%wide.region_10.12_spmd.clone.sunk | while | flops 171179776 | bytes 9515137 | solution.py:225
  2375.0 22.9 fusion.84
  2397.9 48.4 reshape.560
  2466.9 18.4 fusion.101
  2485.3 28.1 pad_maximum_fusion
  2513.4 39.9 reshape.559
  2569.9 36.5 reshape.557
  2609.6 3608.5 %all-reduce.33.cloned.1.call-done = (f32[7680000]{0:T(1024)}, f32[2560000]{0:T(1024)}, f32[10246400]{0:T(1024)}, f32[10240000]{0:T(1024)}) async-done(((f32[7680000]{0:T(1024)}, f32[2560000]{0:T(1024)}, f32[10246400]{0:T(1024)}, f32[10240000]{0:T(1024)}), (f32[7680000]{0:T(1024)}, f32[2560000]{0:T(1024)}, f32[10246400]{0:T(1024)}, f32[10240000]{0:T(1024)})) %all-reduce.33.cloned.1.call-update) | async-done | bytes 122905616
  6239.0 564.4 %all-gather.25.cloned.1.call-done = bf16[8,1,960000]{2,1,0:T(2,128)(2,1)} async-done(((bf16[1,1,960000]{2,1,0:T(2,128)(2,1)}), bf16[8,1,960000]{2,1,0:T(2,128)(2,1)}) %all-gather.25.cloned.1.call-update) | async-done | bytes 15360016 | tf_op jit(solution)/shard_map/all_gather | solution.py:180
  6803.4 325.3 %reduce.27 = bf16[8,960000]{1,0:T(8,128)(2,1)} reduce(bf16[8,1,960000]{2,1,0:T(2,128)(2,1)} %all-gather.25.cloned.1.call-done, bf16[]{:T(256)} %constant.200), dimensions={1}, to_apply=%all-gather.4.reduce_sub_computation | reduce | bytes 30720002 | tf_op jit(solution)/shard_map/all_gather | solution.py:180
  7128.7 33.8 reshape.632
  7162.6 25.2 reshape.556
  7190.0 17.3 fusion.60
  7216.8 36.4 all-reduce.18
  (508 shorter events, 559.9 us)
Async XLA Ops:
  7.2 8.7 copy-start.17
  7.2 48.6 all-gather.19.cloned.1.call-start
  13.5 1022.6 %all-reduce.29.cloned.1.call-start = ((), (), s32[]{:S(2)}) async-start(), calls=%async_computation.7 | async-start | bytes 5124096
  15.8 15.3 copy-start.20
  23.3 1060.8 %all-gather.23.cloned.1.call-start = ((), (), s32[]{:S(2)}) async-start(), calls=%async_computation.11 | async-start | bytes 6400000 | tf_op jit(solution)/shard_map/all_gather | solution.py:107
  31.1 1076.3 %all-gather.21.cloned.1.call-start = ((), (), s32[]{:S(2)}) async-start(), calls=%async_computation.10 | async-start | bytes 11520000 | tf_op jit(solution)/shard_map/all_gather | solution.py:113
  51.5 1111.4 %all-gather.13.cloned.1.call-start = ((), (), s32[]{:S(2)}) async-start(), calls=%async_computation.2 | async-start | bytes 4096000 | tf_op jit(solution)/shard_map/all_gather | solution.py:142
  92.9 309.4 %copy-start.37 = (bf16[200]{0:T(256)(128)(2,1)S(1)}, bf16[200]{0:T(256)(128)(2,1)}, u32[]{:S(2)}) copy-start(bf16[200]{0:T(256)(128)(2,1)} %param.21) | copy-start | bytes 1204
  92.9 309.7 %copy-start.38 = (bf16[200]{0:T(256)(128)(2,1)S(1)}, bf16[200]{0:T(256)(128)(2,1)}, u32[]{:S(2)}) copy-start(bf16[200]{0:T(256)(128)(2,1)} %param.20) | copy-start | bytes 1204
  92.9 402.5 %copy-start.2 = (bf16[1,256,1600]{1,2,0:T(8,128)(2,1)S(1)}, bf16[1,256,1600]{1,2,0:T(8,128)(2,1)}, u32[]{:S(2)}) copy-start(bf16[1,256,1600]{1,2,0:T(8,128)(2,1)} %param.13) | copy-start | bytes 2457604
  97.2 46.9 collective-permute-start
  145.4 95.9 %collective-permute-start.1 = (bf16[960000]{0:T(1024)(128)(2,1)S(1)}, bf16[960000]{0:T(1024)(128)(2,1)S(1)}, u32[]{:S(2)}, u32[]{:S(2)}) collective-permute-start(bf16[960000]{0:T(1024)(128)(2,1)S(1)} %collective-permute-done), channel_id=1, source_target_pairs={{0,4},{4,8},{8,12},{12,16},{16,20},{20,24},{24,28},{28,0},{1,5},{5... | collective-permute-start | bytes 5760008 | tf_op jit(solution)/shard_map/ppermute | solution.py:18
  145.4 98.3 %collective-permute-start.4 = (bf16[960000]{0:T(1024)(128)(2,1)}, bf16[960000]{0:T(1024)(128)(2,1)S(1)}, u32[]{:S(2)}, u32[]{:S(2)}) collective-permute-start(bf16[960000]{0:T(1024)(128)(2,1)} %reshape.580), channel_id=1, source_target_pairs={{0,28},{4,0},{8,4},{12,8},{16,12},{20,16},{24,20},{28,24},{1,29},{... | collective-permute-start | bytes 5760008 | tf_op jit(solution)/shard_map/ppermute | solution.py:20
  241.2 135.2 %copy-start.8 = (bf16[960000]{0:T(1024)(128)(2,1)}, bf16[960000]{0:T(1024)(128)(2,1)S(1)}, u32[]{:S(2)}) copy-start(bf16[960000]{0:T(1024)(128)(2,1)S(1)} %collective-permute-done.1) | copy-start | bytes 5760004
  241.2 125.5 %collective-permute-start.2 = (bf16[960000]{0:T(1024)(128)(2,1)S(1)}, bf16[960000]{0:T(1024)(128)(2,1)}, u32[]{:S(2)}, u32[]{:S(2)}) collective-permute-start(bf16[960000]{0:T(1024)(128)(2,1)S(1)} %collective-permute-done.1), channel_id=1, source_target_pairs={{0,4},{4,8},{8,12},{12,16},{16,20},{20,24},{24,28},{28,0},{1,5},{5... | collective-permute-start | bytes 5760008 | tf_op jit(solution)/shard_map/ppermute | solution.py:18
  245.0 131.4 %collective-permute-start.5 = (bf16[960000]{0:T(1024)(128)(2,1)S(1)}, bf16[960000]{0:T(1024)(128)(2,1)}, u32[]{:S(2)}, u32[]{:S(2)}) collective-permute-start(bf16[960000]{0:T(1024)(128)(2,1)S(1)} %collective-permute-done.4), channel_id=1, source_target_pairs={{0,28},{4,0},{8,4},{12,8},{16,12},{20,16},{24,20},{28,24},{1,29},{... | collective-permute-start | bytes 5760008 | tf_op jit(solution)/shard_map/ppermute | solution.py:20
  366.8 130.4 %collective-permute-start.3 = (bf16[960000]{0:T(1024)(128)(2,1)}, bf16[960000]{0:T(1024)(128)(2,1)}, u32[]{:S(2)}, u32[]{:S(2)}) collective-permute-start(bf16[960000]{0:T(1024)(128)(2,1)} %collective-permute-done.2), channel_id=1, source_target_pairs={{0,4},{4,8},{8,12},{12,16},{16,20},{20,24},{24,28},{28,0},{1,5},{5... | collective-permute-start | bytes 5760008 | tf_op jit(solution)/shard_map/ppermute | solution.py:18
  376.4 330.6 %collective-permute-start.6 = (bf16[960000]{0:T(1024)(128)(2,1)}, bf16[960000]{0:T(1024)(128)(2,1)}, u32[]{:S(2)}, u32[]{:S(2)}) collective-permute-start(bf16[960000]{0:T(1024)(128)(2,1)} %collective-permute-done.5), channel_id=1, source_target_pairs={{0,28},{4,0},{8,4},{12,8},{16,12},{20,16},{24,20},{28,24},{1,29},{... | collective-permute-start | bytes 5760008 | tf_op jit(solution)/shard_map/ppermute | solution.py:20
  495.6 519.3 %copy-start.23 = (f32[256]{0:T(256)}, f32[256]{0:T(256)S(1)}, u32[]{:S(2)}) copy-start(f32[256]{0:T(256)S(1)} %broadcast_multiply_fusion.1) | copy-start | bytes 3076
  495.9 519.0 %copy-start.25 = (f32[256]{0:T(256)}, f32[256]{0:T(256)S(1)}, u32[]{:S(2)}) copy-start(f32[256]{0:T(256)S(1)} %fusion.95) | copy-start | bytes 3076
  497.2 517.7 %copy-start.18 = (f32[1600]{0:T(1024)}, f32[1600]{0:T(1024)S(1)}, u32[]{:S(2)}) copy-start(f32[1600]{0:T(1024)S(1)} %get-tuple-element.229) | copy-start | bytes 19204
  497.2 517.7 %copy-start.21 = (f32[1600]{0:T(1024)}, f32[1600]{0:T(1024)S(1)}, u32[]{:S(2)}) copy-start(f32[1600]{0:T(1024)S(1)} %get-tuple-element.228) | copy-start | bytes 19204
  1032.1 138.0 %all-gather.15.cloned.1.call-start = ((), (), s32[]{:S(2)}) async-start(), calls=%async_computation.3 | async-start | bytes 4096000 | tf_op jit(solution)/shard_map/all_gather | solution.py:143
  1035.4 675.3 %all-reduce.31.cloned.1.call-start = ((), (), s32[]{:S(2)}) async-start(), calls=%async_computation.8 | async-start | bytes 40988672
  1083.6 1020.5 %all-gather.17.cloned.1.call-start = ((), (), s32[]{:S(2)}) async-start(), calls=%async_computation.4 | async-start | bytes 23040000 | tf_op jit(solution)/shard_map/all_gather | solution.py:115
  1106.6 1446.7 %reduce-scatter.3.cloned.1.call-start = ((), (), s32[]{:S(2)}) async-start(), calls=%async_computation.5 | async-start | bytes 8192000 | tf_op jit(solution)/shard_map/reduce_scatter | solution.py:230
  1107.4 1267.6 %copy-start.35 = (bf16[256]{0:T(256)(128)(2,1)}, bf16[256]{0:T(256)(128)(2,1)S(1)}, u32[]{:S(2)}) copy-start(bf16[256]{0:T(256)(128)(2,1)S(1)} %compare_convert_fusion) | copy-start | bytes 1540
  1257.3 5.2 copy-start.12
  1262.5 1204.4 %copy-start = (f32[1,256,1600]{1,2,0:T(8,128)}, f32[1,256,1600]{1,2,0:T(8,128)S(1)}, u32[]{:S(2)}) copy-start(f32[1,256,1600]{1,2,0:T(8,128)S(1)} %get-tuple-element.235) | copy-start | bytes 4915204
  1776.3 361.7 %copy-start.9 = (bf16[1,256,1600]{1,2,0:T(8,128)(2,1)S(1)}, bf16[1,256,1600]{1,2,0:T(8,128)(2,1)}, u32[]{:S(2)}) copy-start(bf16[1,256,1600]{1,2,0:T(8,128)(2,1)} %param.14) | copy-start | bytes 2457604
  2165.9 5.7 copy-start.4
  2165.9 5.7 copy-start.29
  2374.3 180.6 %reduce-scatter.5.cloned.1.call-start = ((), (), s32[]{:S(2)}) async-start(), calls=%async_computation.6 | async-start | bytes 8192000 | tf_op jit(solution)/shard_map/reduce_scatter | solution.py:231
  2374.9 3843.2 %all-reduce.33.cloned.1.call-start = ((), (), s32[]{:S(2)}) async-start(), calls=%async_computation.13 | async-start | bytes 245817344
  2397.9 48.4 copy-start.13
  2554.9 15.0 copy-start.14
  2557.0 13.0 copy-start.15
  2606.5 4196.9 %all-gather.25.cloned.1.call-start = ((), (), s32[]{:S(2)}) async-start(), calls=%async_computation.12 | async-start | bytes 34560000 | tf_op jit(solution)/shard_map/all_gather | solution.py:180
  2607.1 4656.6 %all-reduce.35.cloned.1.call-start = ((), (), s32[]{:S(2)}) async-start(), calls=%async_computation.14 | async-start | bytes 30736384
  7162.5 27.4 copy-start.27
  7162.5 27.4 copy-start.28
  7162.5 27.4 copy-start.34
  7162.5 27.5 copy-start.1
  7162.5 27.4 copy-start.33
  7207.3 8.5 copy-start.32
  7215.5 44.9 copy-start.10
  7215.5 44.9 copy-start.30
  7215.5 44.9 copy-start.36
  (11 other events, 29.5 us)
Sparse Core Ops, SparseCore 0:
  13.6 42.0 all-gather.18
  58.1 59.2 all-reduce.28
  119.6 39.7 all-gather.22
  161.7 309.5 all-gather.20
  1032.2 28.5 all-gather.12
  1062.8 29.7 all-gather.14
  1097.2 613.4 all-reduce.30
  1712.3 391.6 all-gather.16
  2374.5 60.0 reduce-scatter.2
  2436.9 60.1 reduce-scatter.4
  2606.6 3611.4 all-reduce.32
  6219.5 583.8 all-gather.24
  6806.8 267.0 all-reduce.34
